TPU v7x, 32 devices: a whole 2x2x4 slice. The times are simulated.
32 devices in a mesh: head: 4 (over y, x), ctx: 8 (over z, core).
Axes of the slice: x: 2, y: 2, z: 4, core: 2. Of those that a mesh axis runs over, the one named last changes fastest.
Arguments:
- query_in: bfloat16 [4096, 4096], P(('ctx', 'head')), may hold values from -6 to 6
- key_in: bfloat16 [4096, 1024], P(('ctx', 'head')), may hold values from -6 to 6
- value_in: bfloat16 [4096, 1024], P(('ctx', 'head')), may hold values from -6 to 6
- attn_out: bfloat16 [4096, 4096], P(('ctx', 'head')), may hold values from -2 to 2
- out_grad: bfloat16 [4096, 4096], P(('ctx', 'head')), may hold values from -6 to 6
- log_norm: float32 [4096, 32], P(('ctx', 'head')), may hold values from 4 to 8
- doc_ids: int32 [4096], replicated, may hold values from 0 to 15, never falling along the last dimension, each value on 1 to 512 neighbouring positions
Outputs:
- query_grad: bfloat16 [4096, 4096], P(('ctx', 'head'))
- key_grad: bfloat16 [4096, 1024], P(('ctx', 'head'))
- value_grad: bfloat16 [4096, 1024], P(('ctx', 'head'))
Inputs may be any that keep to these rules, and one draw needn't show every extreme that they name: `doc_ids`: document numbers never fall along the sequence and start at 0; every document has 1 to 512 tokens and one has exactly 512.
All inputs are finite; a program needn't handle non-finite values.
Results may differ from a plain program's by a relative error of at most 0.0049.
Values may be sent and summed in bfloat16 or wider, within the bound.
No kernel may reach another device: no remote copies, remote signals or barrier semaphores. Data moves between devices by JAX's collectives and lax.ppermute only.
A program may use at most 128 MiB of HBM per device.

v0:
```python
import jax
import jax.numpy as jnp
from jax import lax
from jax.sharding import PartitionSpec as P

HEAD_DIM = 128


def shifted(value, axis, by):
    count = lax.axis_size(axis)
    pairs = [(i, i + by) for i in range(count) if 0 <= i + by < count]
    return lax.ppermute(value, axis, pairs)


def shifted_2(value, axis, by):
    count = lax.axis_size(axis)
    return lax.ppermute(value, axis, [(i, (i + by) % count) for i in range(count)])


def block_terms(
    query_rows,
    dout_rows,
    norm_rows,
    delta_rows,
    query_ids,
    query_start,
    key_rows,
    value_rows,
    key_ids,
    key_start,
):
    r = query_rows.shape[0]
    c = key_rows.shape[0]
    kv_local = key_rows.shape[1] // HEAD_DIM
    heads_local = query_rows.shape[1] // HEAD_DIM
    group = heads_local // kv_local
    scaling = HEAD_DIM ** (-0.5)
    query_heads = query_rows.reshape(r, kv_local, group, HEAD_DIM)
    dout_heads = dout_rows.reshape(r, kv_local, group, HEAD_DIM)
    key_heads = key_rows.reshape(c, kv_local, HEAD_DIM)
    value_heads = value_rows.reshape(c, kv_local, HEAD_DIM)
    scores = (
        jnp.einsum("qgjd,kgd->gjqk", query_heads, key_heads, preferred_element_type=jnp.float32)
        * scaling
    )
    norm_cols = jnp.transpose(norm_rows.reshape(r, kv_local, group), (1, 2, 0))[..., None]
    delta_cols = jnp.transpose(delta_rows.reshape(r, kv_local, group), (1, 2, 0))[..., None]
    query_pos = query_start + jnp.arange(r, dtype=jnp.int32)
    key_pos = key_start + jnp.arange(c, dtype=jnp.int32)
    allowed = (query_ids[:, None] == key_ids[None, :]) & (query_pos[:, None] >= key_pos[None, :])
    weights = jnp.where(allowed, jnp.exp(scores - norm_cols), 0.0)
    weights_low = weights.astype(jnp.bfloat16)
    grad_value = jnp.einsum(
        "gjqk,qgjd->kgd", weights_low, dout_heads, preferred_element_type=jnp.float32
    )
    prob_grad = jnp.einsum(
        "qgjd,kgd->gjqk", dout_heads, value_heads, preferred_element_type=jnp.float32
    )
    score_grad = (weights * (prob_grad - delta_cols)).astype(jnp.bfloat16)
    grad_query = (
        jnp.einsum("gjqk,kgd->qgjd", score_grad, key_heads, preferred_element_type=jnp.float32)
        * scaling
    )
    grad_key = (
        jnp.einsum("gjqk,qgjd->kgd", score_grad, query_heads, preferred_element_type=jnp.float32)
        * scaling
    )
    return (
        grad_query.reshape(r, heads_local * HEAD_DIM),
        grad_key.reshape(c, kv_local * HEAD_DIM),
        grad_value.reshape(c, kv_local * HEAD_DIM),
    )


def head_delta(dout_rows, output_rows):
    row_count = dout_rows.shape[0]
    product = dout_rows.astype(jnp.float32) * output_rows.astype(jnp.float32)
    return jnp.sum(product.reshape(row_count, -1, HEAD_DIM), axis=2)


def local(query_in, key_in, value_in, attn_out, out_grad, log_norm, doc_ids):
    query_rows, key_rows, value_rows, dout_rows, output_rows = (
        lax.all_to_all(query_in, "head", split_axis=1, concat_axis=0, tiled=True),
        lax.all_to_all(key_in, "head", split_axis=1, concat_axis=0, tiled=True),
        lax.all_to_all(value_in, "head", split_axis=1, concat_axis=0, tiled=True),
        lax.all_to_all(attn_out, "head", split_axis=1, concat_axis=0, tiled=True),
        lax.all_to_all(out_grad, "head", split_axis=1, concat_axis=0, tiled=True),
    )
    norm_rows = lax.all_to_all(log_norm, "head", split_axis=1, concat_axis=0, tiled=True)
    dout_rows, output_rows = (output_rows, dout_rows)
    delta_rows = head_delta(dout_rows, output_rows)
    row_count = query_rows.shape[0]
    cycle_size = lax.axis_size("ctx")
    my_index = lax.axis_index("ctx")
    my_start = my_index * row_count
    visits = min(cycle_size, row_count // row_count + 1)

    def ids_at(start):
        return lax.dynamic_slice_in_dim(doc_ids, start, row_count)

    my_ids = ids_at(my_start)
    query_zero = jnp.zeros(query_rows.shape, jnp.float32)
    key_zero = jnp.zeros(key_rows.shape, jnp.float32)

    def skipped(_):
        return (query_zero, key_zero, key_zero)

    key_value = jnp.stack((key_rows, value_rows))

    def visit_block(held_pair, grad_pair, source):
        key_start = source * row_count

        def compute(_):
            return block_terms(
                query_rows,
                dout_rows,
                norm_rows,
                delta_rows,
                my_ids,
                my_start,
                held_pair[0],
                held_pair[1],
                ids_at(key_start),
                key_start,
            )

        grad_query, grad_key, grad_value = lax.cond(source <= my_index, compute, skipped, 0)
        return (grad_query, grad_pair + jnp.stack((grad_key, grad_value)))

    def cycle_turn(turn_index, carry):
        held_pair, grad_pair, query_total = carry
        following = shifted(held_pair, "ctx", 1)
        grad_query, grad_pair = visit_block(
            held_pair, grad_pair, (my_index - turn_index) % cycle_size
        )
        grad_pair = shifted_2(grad_pair, "ctx", 1)
        return (following, grad_pair, query_total + grad_query)

    start = (key_value, jnp.zeros(key_value.shape, jnp.float32), query_zero)
    held_pair, grad_pair, query_total = lax.fori_loop(0, visits - 1, cycle_turn, start)
    grad_query, grad_pair = visit_block(
        held_pair, grad_pair, (my_index - (visits - 1)) % cycle_size
    )
    grad_pair = shifted_2(grad_pair.astype(jnp.bfloat16), "ctx", 1 - visits).astype(grad_pair.dtype)
    query_total = query_total + grad_query
    key_total = grad_pair[0]
    value_total = grad_pair[1]
    query_grad, key_grad, value_grad = (
        lax.all_to_all(
            query_total.astype(jnp.bfloat16), "head", split_axis=0, concat_axis=1, tiled=True
        ),
        lax.all_to_all(
            key_total.astype(jnp.bfloat16), "head", split_axis=0, concat_axis=1, tiled=True
        ),
        lax.all_to_all(
            value_total.astype(jnp.bfloat16), "head", split_axis=0, concat_axis=1, tiled=True
        ),
    )
    return (query_grad, key_grad, value_grad)


def solution(mesh):
    in_specs = (
        P(("ctx", "head"), None),
        P(("ctx", "head"), None),
        P(("ctx", "head"), None),
        P(("ctx", "head"), None),
        P(("ctx", "head"), None),
        P(("ctx", "head"), None),
        P(),
    )
    out_specs = (P(("ctx", "head"), None), P(("ctx", "head"), None), P(("ctx", "head"), None))
    return jax.shard_map(local, mesh=mesh, in_specs=in_specs, out_specs=out_specs, check_vma=False)
```

profile of v0, /device:TPU:8, one launch (start us, length us, event | category | flops | bytes accessed | tf_op | source)
XLA Modules:
  0.0 171.9 jit_solution(2658840993720488320)
XLA Ops:
  2.5 3.7 %all-to-all-start = ((bf16[128,4,256]{0,2,1:T(8,128)(2,1)}), bf16[128,4,256]{0,2,1:T(8,128)(2,1)S(1)}, u32[]{:S(2)}, u32[]{:S(2)}) async-start(bf16[128,4,256]{0,2,1:T(8,128)(2,1)} %bitcast.44), calls=%async_computation | async-start | bytes 524288 | tf_op jit(solution)/shard_map/all_to_all | solution.py:84
  8.0 3.6 %all-to-all-done = bf16[128,4,256]{0,2,1:T(8,128)(2,1)S(1)} async-done(((bf16[128,4,256]{0,2,1:T(8,128)(2,1)}), bf16[128,4,256]{0,2,1:T(8,128)(2,1)S(1)}, u32[]{:S(2)}, u32[]{:S(2)}) %all-to-all-start) | async-done | bytes 262176 | tf_op jit(solution)/shard_map/all_to_all | solution.py:84
  11.6 3.4 %all-to-all-start.1 = ((bf16[128,4,256]{0,2,1:T(8,128)(2,1)}), bf16[128,4,256]{0,2,1:T(8,128)(2,1)S(1)}, u32[]{:S(2)}, u32[]{:S(2)}) async-start(bf16[128,4,256]{0,2,1:T(8,128)(2,1)} %bitcast.47), calls=%async_computation.1 | async-start | bytes 524288 | tf_op jit(solution)/shard_map/all_to_all | solution.py:85
  15.0 2.3 %copy.135 = bf16[128,4096]{0,1:T(8,128)(2,1)} copy(bf16[128,4096]{1,0:T(8,128)(2,1)} %param.14) | data formatting | bytes 2097152 | tf_op args[3]
  17.3 3.1 %all-to-all-done.1 = bf16[128,4,256]{0,2,1:T(8,128)(2,1)S(1)} async-done(((bf16[128,4,256]{0,2,1:T(8,128)(2,1)}), bf16[128,4,256]{0,2,1:T(8,128)(2,1)S(1)}, u32[]{:S(2)}, u32[]{:S(2)}) %all-to-all-start.1) | async-done | bytes 262176 | tf_op jit(solution)/shard_map/all_to_all | solution.py:85
  21.1 3.5 %all-to-all-start.5 = ((bf16[128,4,1024]{0,2,1:T(8,128)(2,1)}), bf16[128,4,1024]{0,2,1:T(8,128)(2,1)S(1)}, u32[]{:S(2)}, u32[]{:S(2)}) async-start(bf16[128,4,1024]{0,2,1:T(8,128)(2,1)} %bitcast.59), calls=%async_computation.5 | async-start | bytes 2097152 | tf_op jit(solution)/shard_map/all_to_all | solution.py:86
  24.6 2.3 %copy.133 = bf16[128,4096]{0,1:T(8,128)(2,1)} copy(bf16[128,4096]{1,0:T(8,128)(2,1)} %param.15) | data formatting | bytes 2097152 | tf_op args[4]
  26.9 9.0 %all-to-all-done.5 = bf16[128,4,1024]{0,2,1:T(8,128)(2,1)S(1)} async-done(((bf16[128,4,1024]{0,2,1:T(8,128)(2,1)}), bf16[128,4,1024]{0,2,1:T(8,128)(2,1)S(1)}, u32[]{:S(2)}, u32[]{:S(2)}) %all-to-all-start.5) | async-done | bytes 1048608 | tf_op jit(solution)/shard_map/all_to_all | solution.py:86
  35.9 3.5 %all-to-all-start.4 = ((bf16[128,4,1024]{0,2,1:T(8,128)(2,1)}), bf16[128,4,1024]{0,2,1:T(8,128)(2,1)S(1)}, u32[]{:S(2)}, u32[]{:S(2)}) async-start(bf16[128,4,1024]{0,2,1:T(8,128)(2,1)} %bitcast.56), calls=%async_computation.4 | async-start | bytes 2097152 | tf_op jit(solution)/shard_map/all_to_all | solution.py:87
  40.7 11.8 %all-to-all-done.4 = bf16[128,4,1024]{0,2,1:T(8,128)(2,1)S(1)} async-done(((bf16[128,4,1024]{0,2,1:T(8,128)(2,1)}), bf16[128,4,1024]{0,2,1:T(8,128)(2,1)S(1)}, u32[]{:S(2)}, u32[]{:S(2)}) %all-to-all-start.4) | async-done | bytes 1048608 | tf_op jit(solution)/shard_map/all_to_all | solution.py:87
  52.5 3.5 %all-to-all-start.2 = ((bf16[128,4,1024]{0,2,1:T(8,128)(2,1)}), bf16[128,4,1024]{0,2,1:T(8,128)(2,1)S(1)}, u32[]{:S(2)}, u32[]{:S(2)}) async-start(bf16[128,4,1024]{0,2,1:T(8,128)(2,1)} %bitcast.177), calls=%async_computation.2 | async-start | bytes 2097152 | tf_op jit(solution)/shard_map/all_to_all | solution.py:83
  62.4 6.7 %all-to-all-done.2 = bf16[128,4,1024]{0,2,1:T(8,128)(2,1)S(1)} async-done(((bf16[128,4,1024]{0,2,1:T(8,128)(2,1)}), bf16[128,4,1024]{0,2,1:T(8,128)(2,1)S(1)}, u32[]{:S(2)}, u32[]{:S(2)}) %all-to-all-start.2) | async-done | bytes 1048608 | tf_op jit(solution)/shard_map/all_to_all | solution.py:83
  69.2 3.3 %all-to-all-start.3 = ((f32[128,4,8]{0,2,1:T(8,128)}), f32[128,4,8]{0,2,1:T(8,128)S(1)}, u32[]{:S(2)}, u32[]{:S(2)}) async-start(f32[128,4,8]{0,2,1:T(8,128)} %bitcast.53), calls=%async_computation.3 | async-start | bytes 32768 | tf_op jit(solution)/shard_map/all_to_all | solution.py:89
  77.1 18.2 %conditional.2 = (f32[512,1024]{0,1:T(8,128)}, f32[1,512,256]{1,2,0:T(8,128)}, f32[1,512,256]{1,2,0:T(8,128)}) conditional(s32[]{:T(128)} %convert_element_type.49, () %tuple.34, (s32[512]{0:T(512)S(1)}, s32[]{:T(128)}, s32[4096]{0:T(1024)}, s32[]{:T(128)}, bf16[2,512,256]{2,1,0:T(8,128)(2,1)}, /*index=5*/bf16[512,1024]{1,0:T(8,128)(2,1)S(1)}, ...), branch_computations={%region_1.2_spmd, %region_2.3_spmd} | conditional | flops 2706768896 | bytes 60457152 | solution.py:127
  83.0 2.3 %fusion.26 = f32[2,512,512,4]{2,1,3,0:T(8,128)S(1)} fusion(bf16[512,2,128,1]{0,2,3,1:T(8,128)(2,1)} %bitcast.179, bf16[512,2,4,128]{0,3,2,1:T(8,128)(2,1)S(1)} %bitcast.171), kind=kOutput, calls=%fused_computation.43 | convolution fusion | flops 536870912 | bytes 9699328 | tf_op jit(solution)/shard_map/while/body/eval_jaxpr/cond/branch_1_fun/qgjd,kgd->gjqk/dot_general | solution.py:43
  85.3 2.7 %fusion.5 = f32[2,512,128,1]{1,2,3,0:T(8,128)} fusion(bf16[512,2,4,128]{0,3,2,1:T(8,128)(2,1)S(1)} %bitcast.184, f32[2,512,512,4]{2,1,3,0:T(8,128)S(1)} %fusion.26, f32[2,4,512]{2,1,0:T(4,128)S(1)} %bitcast.198, pred[512,512]{0,1:T(8,128)(4,1)S(1)} %copy-done.7), kind=kOutput, calls=%fused_computation.7 | convolution fusion | flops 545259520 | bytes 10240000 | tf_op jit(solution)/shard_map/while/body/eval_jaxpr/cond/branch_1_fun/gjqk,qgjd->kgd/dot_general | solution.py:53
  88.0 3.0 %fusion.1 = bf16[2,4,512,512]{2,3,1,0:T(8,128)(2,1)S(1)} fusion(f32[2,512,512,4]{2,1,3,0:T(8,128)S(1)} %fusion.26, f32[2,4,512]{2,1,0:T(4,128)S(1)} %bitcast.196, f32[2,4,512]{2,1,0:T(4,128)S(1)} %bitcast.199, pred[512,512]{0,1:T(8,128)(4,1)S(1)} %copy-done.7, bf16[512,2,128,1]{0,2,3,1:T(8,128)(2,1)S(1)} %bitcast.192, bf16[512,2,4,128]{0,3,2,1:T(8,128)(2,1)S(1)} %bitcast.185), kind=kOutput, calls=%fused_computation.2 | convolution fusion | flops 549453824 | bytes 14188544 | tf_op jit(solution)/shard_map/while/body/eval_jaxpr/cond/branch_1_fun/qgjd,kgd->gjqk/dot_general | solution.py:56
  91.0 2.3 %fusion.8 = f32[2,512,128]{1,2,0:T(8,128)} fusion(bf16[2,4,512,512]{2,3,1,0:T(8,128)(2,1)S(1)} %fusion.1, bf16[512,2,4,128]{0,3,2,1:T(8,128)(2,1)S(1)} %bitcast.172), kind=kOutput, calls=%fused_computation.11 | convolution fusion | flops 537001984 | bytes 5767168 | tf_op jit(solution)/shard_map/while/body/eval_jaxpr/cond/branch_1_fun/gjqk,qgjd->kgd/dot_general | solution.py:65
  95.3 2.3 %pad_maximum_fusion = f32[2,512,256]{1,2,0:T(8,128)} fusion(f32[1,512,256]{1,2,0:T(8,128)} %get-tuple-element.113, f32[1,512,256]{1,2,0:T(8,128)} %get-tuple-element.112), kind=kLoop, calls=%fused_computation.36 | loop fusion | flops 262144 | bytes 2097152 | tf_op jit(solution)/shard_map/while/body/eval_jaxpr/stack | solution.py:128
  97.6 3.6 %collective-permute-start = (bf16[2,512,256]{2,1,0:T(8,128)(2,1)}, bf16[2,512,256]{2,1,0:T(8,128)(2,1)S(1)}, u32[]{:S(2)}, u32[]{:S(2)}) collective-permute-start(bf16[2,512,256]{2,1,0:T(8,128)(2,1)} %pad_maximum_fusion.1), channel_id=1, source_target_pairs={{0,1},{1,2},{2,3},{3,4},{4,5},{5,6},{6,7},{8,9},{9,10},{10,11},{11... | collective-permute-start | bytes 1572872 | tf_op jit(solution)/shard_map/while/body/eval_jaxpr/ppermute | solution.py:12
  101.2 16.4 %collective-permute-done = bf16[2,512,256]{2,1,0:T(8,128)(2,1)S(1)} collective-permute-done((bf16[2,512,256]{2,1,0:T(8,128)(2,1)}, bf16[2,512,256]{2,1,0:T(8,128)(2,1)S(1)}, u32[]{:S(2)}, u32[]{:S(2)}) %collective-permute-start) | collective-permute-done | bytes 524320 | tf_op jit(solution)/shard_map/while/body/eval_jaxpr/ppermute | solution.py:12
  117.7 14.9 %conditional.3 = (f32[512,1024]{0,1:T(8,128)}, f32[1,512,256]{1,2,0:T(8,128)}, f32[1,512,256]{1,2,0:T(8,128)S(1)}) conditional(s32[]{:T(128)} %convert_element_type.53, () %tuple.36, (s32[512]{0:T(512)S(1)}, s32[]{:T(128)}, s32[4096]{0:T(1024)}, s32[]{:T(128)}, bf16[2,512,256]{2,1,0:T(8,128)(2,1)S(1)}, /*index=5*/bf16[512,1024]{1,0:T(8,128)(2,1)S(1)}, ...), branch_computations={%region_3.4_spmd, %region_4.5_spmd} | conditional | flops 2706768896 | bytes 59408520 | solution.py:127
  125.2 3.0 %fusion.12 = bf16[2,4,512,512]{2,3,1,0:T(8,128)(2,1)S(1)} fusion(f32[2,512,512,4]{2,1,3,0:T(8,128)S(1)} %fusion.27, f32[2,4,512]{2,1,0:T(4,128)S(1)} %bitcast.197, f32[2,4,512]{2,1,0:T(4,128)S(1)} %bitcast.201, pred[512,512]{0,1:T(8,128)(4,1)S(1)} %compare_and_fusion.1, bf16[512,2,128,1]{0,2,3,1:T(8,128)(2,1)S(1)} %bitcast.193, ...), kind=kOutput, calls=%fused_computation.19 | convolution fusion | flops 549453824 | bytes 14188544 | tf_op jit(solution)/shard_map/cond/branch_1_fun/qgjd,kgd->gjqk/dot_general | solution.py:56
  128.2 2.3 %fusion.19 = f32[2,512,128]{1,2,0:T(8,128)} fusion(bf16[2,4,512,512]{2,3,1,0:T(8,128)(2,1)S(1)} %fusion.12, bf16[512,2,4,128]{0,3,2,1:T(8,128)(2,1)S(1)} %bitcast.174), kind=kOutput, calls=%fused_computation.28 | convolution fusion | flops 537001984 | bytes 5767168 | tf_op jit(solution)/shard_map/cond/branch_1_fun/gjqk,qgjd->kgd/dot_general | solution.py:65
  132.5 2.6 %add_convert_fusion = bf16[512,1024]{0,1:T(8,128)(2,1)S(1)} fusion(f32[512,1024]{0,1:T(8,128)} %get-tuple-element.110, f32[512,1024]{0,1:T(8,128)} %get-tuple-element.111), kind=kLoop, calls=%fused_computation.35 | loop fusion | flops 1048576 | bytes 5242880 | tf_op jit(solution)/shard_map/convert_element_type | solution.py:150
  136.4 3.7 %all-to-all-start.6 = ((bf16[4,128,1024]{2,1,0:T(8,128)(2,1)}), bf16[4,128,1024]{2,1,0:T(8,128)(2,1)S(1)}, u32[]{:S(2)}, u32[]{:S(2)}) async-start(bf16[4,128,1024]{2,1,0:T(8,128)(2,1)} %bitcast.64), calls=%async_computation.6 | async-start | bytes 2097152 | tf_op jit(solution)/shard_map/all_to_all | solution.py:149
  141.8 6.7 %collective-permute-done.2 = bf16[2,512,256]{1,2,0:T(8,128)(2,1)S(1)} collective-permute-done((bf16[2,512,256]{1,2,0:T(8,128)(2,1)S(1)}, bf16[2,512,256]{1,2,0:T(8,128)(2,1)S(1)}, u32[]{:S(2)}, u32[]{:S(2)}) %collective-permute-start.2) | collective-permute-done | bytes 524320 | tf_op jit(solution)/shard_map/ppermute | solution.py:17
  149.3 4.0 %all-to-all-done.6 = bf16[4,128,1024]{2,1,0:T(8,128)(2,1)S(1)} async-done(((bf16[4,128,1024]{2,1,0:T(8,128)(2,1)}), bf16[4,128,1024]{2,1,0:T(8,128)(2,1)S(1)}, u32[]{:S(2)}, u32[]{:S(2)}) %all-to-all-start.6) | async-done | bytes 1048608 | tf_op jit(solution)/shard_map/all_to_all | solution.py:149
  153.3 3.4 %all-to-all-start.8 = ((bf16[4,128,256]{2,1,0:T(8,128)(2,1)}), bf16[4,128,256]{2,1,0:T(8,128)(2,1)S(1)}, u32[]{:S(2)}, u32[]{:S(2)}) async-start(bf16[4,128,256]{2,1,0:T(8,128)(2,1)} %bitcast.70), calls=%async_computation.8 | async-start | bytes 524288 | tf_op jit(solution)/shard_map/all_to_all | solution.py:155
  157.6 4.5 %all-to-all-done.8 = bf16[4,128,256]{2,1,0:T(8,128)(2,1)S(1)} async-done(((bf16[4,128,256]{2,1,0:T(8,128)(2,1)}), bf16[4,128,256]{2,1,0:T(8,128)(2,1)S(1)}, u32[]{:S(2)}, u32[]{:S(2)}) %all-to-all-start.8) | async-done | bytes 262176 | tf_op jit(solution)/shard_map/all_to_all | solution.py:155
  162.1 3.4 %all-to-all-start.7 = ((bf16[4,128,256]{2,1,0:T(8,128)(2,1)}), bf16[4,128,256]{2,1,0:T(8,128)(2,1)S(1)}, u32[]{:S(2)}, u32[]{:S(2)}) async-start(bf16[4,128,256]{2,1,0:T(8,128)(2,1)} %bitcast.67), calls=%async_computation.7 | async-start | bytes 524288 | tf_op jit(solution)/shard_map/all_to_all | solution.py:152
  168.5 2.3 %all-to-all-done.7 = bf16[4,128,256]{2,1,0:T(8,128)(2,1)S(1)} async-done(((bf16[4,128,256]{2,1,0:T(8,128)(2,1)}), bf16[4,128,256]{2,1,0:T(8,128)(2,1)S(1)}, u32[]{:S(2)}, u32[]{:S(2)}) %all-to-all-start.7) | async-done | bytes 262176 | tf_op jit(solution)/shard_map/all_to_all | solution.py:152
  (70 shorter events, 42.7 us)
Async XLA Ops:
  0.6 38.8 %copy-start.2 = (bf16[128,4096]{1,0:T(8,128)(2,1)S(1)}, bf16[128,4096]{1,0:T(8,128)(2,1)}, u32[]{:S(2)}) copy-start(bf16[128,4096]{1,0:T(8,128)(2,1)} %param.11) | copy-start | bytes 3145732
  2.5 9.1 %all-to-all-start = ((bf16[128,4,256]{0,2,1:T(8,128)(2,1)}), bf16[128,4,256]{0,2,1:T(8,128)(2,1)S(1)}, u32[]{:S(2)}, u32[]{:S(2)}) async-start(bf16[128,4,256]{0,2,1:T(8,128)(2,1)} %bitcast.44), calls=%async_computation | async-start | bytes 524288 | tf_op jit(solution)/shard_map/all_to_all | solution.py:84
  11.6 8.8 %all-to-all-start.1 = ((bf16[128,4,256]{0,2,1:T(8,128)(2,1)}), bf16[128,4,256]{0,2,1:T(8,128)(2,1)S(1)}, u32[]{:S(2)}, u32[]{:S(2)}) async-start(bf16[128,4,256]{0,2,1:T(8,128)(2,1)} %bitcast.47), calls=%async_computation.1 | async-start | bytes 524288 | tf_op jit(solution)/shard_map/all_to_all | solution.py:85
  20.4 0.7 copy-start.5
  21.1 14.8 %all-to-all-start.5 = ((bf16[128,4,1024]{0,2,1:T(8,128)(2,1)}), bf16[128,4,1024]{0,2,1:T(8,128)(2,1)S(1)}, u32[]{:S(2)}, u32[]{:S(2)}) async-start(bf16[128,4,1024]{0,2,1:T(8,128)(2,1)} %bitcast.59), calls=%async_computation.5 | async-start | bytes 2097152 | tf_op jit(solution)/shard_map/all_to_all | solution.py:86
  35.9 16.6 %all-to-all-start.4 = ((bf16[128,4,1024]{0,2,1:T(8,128)(2,1)}), bf16[128,4,1024]{0,2,1:T(8,128)(2,1)S(1)}, u32[]{:S(2)}, u32[]{:S(2)}) async-start(bf16[128,4,1024]{0,2,1:T(8,128)(2,1)} %bitcast.56), calls=%async_computation.4 | async-start | bytes 2097152 | tf_op jit(solution)/shard_map/all_to_all | solution.py:87
  52.5 16.6 %all-to-all-start.2 = ((bf16[128,4,1024]{0,2,1:T(8,128)(2,1)}), bf16[128,4,1024]{0,2,1:T(8,128)(2,1)S(1)}, u32[]{:S(2)}, u32[]{:S(2)}) async-start(bf16[128,4,1024]{0,2,1:T(8,128)(2,1)} %bitcast.177), calls=%async_computation.2 | async-start | bytes 2097152 | tf_op jit(solution)/shard_map/all_to_all | solution.py:83
  69.2 4.9 %copy-start = (bf16[128,4,1024]{0,2,1:T(8,128)(2,1)}, bf16[128,4,1024]{0,2,1:T(8,128)(2,1)S(1)}, u32[]{:S(2)}) copy-start(bf16[128,4,1024]{0,2,1:T(8,128)(2,1)S(1)} %all-to-all-done.2) | copy-start | bytes 3145732
  69.2 7.9 %all-to-all-start.3 = ((f32[128,4,8]{0,2,1:T(8,128)}), f32[128,4,8]{0,2,1:T(8,128)S(1)}, u32[]{:S(2)}, u32[]{:S(2)}) async-start(f32[128,4,8]{0,2,1:T(8,128)} %bitcast.53), calls=%async_computation.3 | async-start | bytes 32768 | tf_op jit(solution)/shard_map/all_to_all | solution.py:89
  82.9 2.4 %copy-start.3 = (bf16[512,1024]{0,1:T(8,128)(2,1)S(1)}, bf16[512,1024]{0,1:T(8,128)(2,1)}, u32[]{:S(2)}) copy-start(bf16[512,1024]{0,1:T(8,128)(2,1)} %copy.139) | copy-start | bytes 3145732 | tf_op jit(solution)/shard_map/while/body/eval_jaxpr/cond
  82.9 2.4 %copy-start.7 = (pred[512,512]{0,1:T(8,128)(4,1)S(1)}, pred[512,512]{0,1:T(8,128)(4,1)}, u32[]{:S(2)}) copy-start(pred[512,512]{0,1:T(8,128)(4,1)} %compare_and_fusion) | copy-start | bytes 786436 | tf_op jit(solution)/shard_map/while/body/eval_jaxpr/cond
  85.3 2.7 %copy-start.8 = (bf16[1,512,256]{1,2,0:T(8,128)(2,1)S(1)}, bf16[1,512,256]{1,2,0:T(8,128)(2,1)}, u32[]{:S(2)}) copy-start(bf16[1,512,256]{1,2,0:T(8,128)(2,1)} %get-tuple-element.158) | copy-start | bytes 786436 | tf_op jit(solution)/shard_map/while/body/eval_jaxpr/cond
  88.0 5.2 %copy-start.1 = (bf16[1,512,256]{1,2,0:T(8,128)(2,1)S(1)}, bf16[1,512,256]{1,2,0:T(8,128)(2,1)}, u32[]{:S(2)}) copy-start(bf16[1,512,256]{1,2,0:T(8,128)(2,1)} %get-tuple-element.159) | copy-start | bytes 786436 | tf_op jit(solution)/shard_map/while/body/eval_jaxpr/cond
  97.6 42.6 %collective-permute-start.1 = (f32[2,512,256]{1,2,0:T(8,128)}, f32[2,512,256]{1,2,0:T(8,128)}, u32[]{:S(2)}, u32[]{:S(2)}) collective-permute-start(f32[2,512,256]{1,2,0:T(8,128)} %pad_maximum_fusion), channel_id=1, source_target_pairs={{0,1},{1,2},{2,3},{3,4},{4,5},{5,6},{6,7},{7,0},{8,9},{9,10},{10,1... | collective-permute-start | bytes 3145736 | tf_op jit(solution)/shard_map/while/body/eval_jaxpr/ppermute | solution.py:17
  97.6 20.0 %collective-permute-start = (bf16[2,512,256]{2,1,0:T(8,128)(2,1)}, bf16[2,512,256]{2,1,0:T(8,128)(2,1)S(1)}, u32[]{:S(2)}, u32[]{:S(2)}) collective-permute-start(bf16[2,512,256]{2,1,0:T(8,128)(2,1)} %pad_maximum_fusion.1), channel_id=1, source_target_pairs={{0,1},{1,2},{2,3},{3,4},{4,5},{5,6},{6,7},{8,9},{9,10},{10,11},{11... | collective-permute-start | bytes 1572872 | tf_op jit(solution)/shard_map/while/body/eval_jaxpr/ppermute | solution.py:12
  117.7 0.9 copy-start.6
  122.0 1.3 copy-start.4
  136.4 16.9 %all-to-all-start.6 = ((bf16[4,128,1024]{2,1,0:T(8,128)(2,1)}), bf16[4,128,1024]{2,1,0:T(8,128)(2,1)S(1)}, u32[]{:S(2)}, u32[]{:S(2)}) async-start(bf16[4,128,1024]{2,1,0:T(8,128)(2,1)} %bitcast.64), calls=%async_computation.6 | async-start | bytes 2097152 | tf_op jit(solution)/shard_map/all_to_all | solution.py:149
  141.7 6.8 %collective-permute-start.2 = (bf16[2,512,256]{1,2,0:T(8,128)(2,1)S(1)}, bf16[2,512,256]{1,2,0:T(8,128)(2,1)S(1)}, u32[]{:S(2)}, u32[]{:S(2)}) collective-permute-start(bf16[2,512,256]{1,2,0:T(8,128)(2,1)S(1)} %fusion.22), channel_id=1, source_target_pairs={{0,7},{1,0},{2,1},{3,2},{4,3},{5,4},{6,5},{7,6},{8,15},{9,8},{10,9... | collective-permute-start | bytes 1572872 | tf_op jit(solution)/shard_map/ppermute | solution.py:17
  153.3 8.8 %all-to-all-start.8 = ((bf16[4,128,256]{2,1,0:T(8,128)(2,1)}), bf16[4,128,256]{2,1,0:T(8,128)(2,1)S(1)}, u32[]{:S(2)}, u32[]{:S(2)}) async-start(bf16[4,128,256]{2,1,0:T(8,128)(2,1)} %bitcast.70), calls=%async_computation.8 | async-start | bytes 524288 | tf_op jit(solution)/shard_map/all_to_all | solution.py:155
  162.1 8.8 %all-to-all-start.7 = ((bf16[4,128,256]{2,1,0:T(8,128)(2,1)}), bf16[4,128,256]{2,1,0:T(8,128)(2,1)S(1)}, u32[]{:S(2)}, u32[]{:S(2)}) async-start(bf16[4,128,256]{2,1,0:T(8,128)(2,1)} %bitcast.67), calls=%async_computation.7 | async-start | bytes 524288 | tf_op jit(solution)/shard_map/all_to_all | solution.py:152
where the time goes:
time: 173 us; the launch traced here: 172 us
  waiting for transfers between devices  68.6 us (40%)
  starting transfers between devices  35.1 us (20%)
  local copies, waits for them, and re-layouts  32.7 us (19%)
  matrix products  22.8 us (13%)
  other arithmetic  11.7 us (7%)
    ppermute x1, waiting for transfers between devices, shifted(): return lax.ppermute(value, axis, pairs)  16.4 us
    unnamed x15, local copies, waits for them, and re-layouts  13.7 us
    all_to_all x1, waiting for transfers between devices, local(): lax.all_to_all(out_grad, 'head', split_axis=1, concat_axis=0, tiled=True)  11.8 us
    all_to_all x1, waiting for transfers between devices, local(): lax.all_to_all(attn_out, 'head', split_axis=1, concat_axis=0, tiled=True)  9.04 us
    all_to_all x1, waiting for transfers between devices, local(): lax.all_to_all(query_in, 'head', split_axis=1, concat_axis=0, tiled=True)  6.73 us
    ppermute x2, waiting for transfers between devices, shifted_2(): lax.ppermute(value, axis, [(i, (i + by) % count) for i in range(count)])  6.69 us
    another operation x8, local copies, waits for them, and re-layouts  6.4 us
    dot_general x2, matrix products, block_terms(): jnp.einsum('qgjd,kgd->gjqk', dout_heads, value_heads, preferred_element_t...  5.95 us
  transfers between devices with their start and end apart: 12, of which 11 were waited for; matrix products, arithmetic and copies ran while one was open for 25% of the time, Pallas kernels for 0%

commit v1 on v0

v1 whole, which is shorter than its diff:
```python
import functools

import jax
import jax.numpy as jnp
from jax import lax
from jax.experimental import pallas as pl
from jax.experimental.pallas import tpu as pltpu
from jax.sharding import PartitionSpec as P

HEAD_DIM = 128
MASKED = -1e30
STEP_HEADS = 4
NT = (((1,), (1,)), ((), ()))
NN = (((1,), (0,)), ((), ()))
TN = (((0,), (0,)), ((), ()))


def dot(a, b, dims):
    return lax.dot_general(a, b, dims, preferred_element_type=jnp.float32)


def source_place(p, c, m):
    if m == 0:
        return p, c - 1
    source = p ^ m
    return source, c - jnp.where(source > p, 1, 0)


def stacked_heads(ref, first, group):
    return jnp.concatenate(
        [ref[:, j * HEAD_DIM : (j + 1) * HEAD_DIM] for j in range(first, first + group)], axis=0
    )


def add_terms(queries, douts, norm_row, delta_row, bias, keys, values, group):
    scaling = HEAD_DIM ** (-0.5)
    rows = bias.shape[1]
    scores = dot(keys, queries, NT) * scaling
    shift = jnp.concatenate([bias] * group, axis=1) - norm_row
    weights = jnp.exp(scores + shift)
    prob_grad = dot(values, douts, NT)
    grad_value = dot(weights.astype(jnp.bfloat16), douts, NN)
    score_grad = (weights * (prob_grad - delta_row)).astype(jnp.bfloat16)
    grad_key = dot(score_grad, queries, NN) * scaling
    grad_query_t = dot(keys, score_grad, TN) * scaling
    grad_query = jnp.concatenate(
        [grad_query_t[:, j * rows : (j + 1) * rows].T for j in range(group)], axis=1
    )
    return grad_query, grad_key, grad_value


def own_kernel(
    group, head_count, q_ref, do_ref, o_ref, norm_ref, ids_ref, k_ref, v_ref,
    dq_ref, dkv_ref, norm_out, delta_out, start_out, bias_ref, norm_t,
):
    g = pl.program_id(0)
    rows = q_ref.shape[0]
    blocks = ids_ref.shape[0]

    @pl.when(g == 0)
    def _():
        me = lax.axis_index("ctx") * head_count + lax.axis_index("head")
        mine = ids_ref[pl.ds(me, 1), :]
        before = jnp.zeros((1, rows), jnp.int32)
        for back in range(min(head_count, blocks - 1) + 1):
            other = jnp.maximum(me - back, 0)
            ids = jnp.broadcast_to(ids_ref[pl.ds(other, 1), :], (rows, rows)).T
            less = jnp.where((ids < mine) & (me >= back), 1, 0)
            before = before + jnp.sum(less, axis=0, keepdims=True)
        first = jnp.maximum(me - head_count, 0) * rows
        start = first + before
        start_out[...] = jnp.broadcast_to(start, start_out.shape)
        key_at = lax.broadcasted_iota(jnp.int32, (rows, rows), 0)
        query_at = lax.broadcasted_iota(jnp.int32, (rows, rows), 1)
        allowed = (key_at + me * rows >= start) & (key_at <= query_at)
        bias_ref[...] = jnp.where(allowed, 0.0, MASKED)
        norm_t[...] = norm_ref[...].T

    for i in range(k_ref.shape[1] // HEAD_DIM):
        deltas = []
        norms = []
        for j in range(i * group, (i + 1) * group):
            cols = slice(j * HEAD_DIM, (j + 1) * HEAD_DIM)
            product = do_ref[:, cols].astype(jnp.float32) * o_ref[:, cols].astype(jnp.float32)
            deltas.append(jnp.sum(product.T, axis=0, keepdims=True))
            norms.append(norm_t[pl.ds(g * (group * norm_out.shape[0]) + j, 1), :])
        delta_row = jnp.concatenate(deltas, axis=1)
        norm_row = jnp.concatenate(norms, axis=1)
        delta_out[i] = delta_row
        norm_out[i] = norm_row
        at = slice(i * HEAD_DIM, (i + 1) * HEAD_DIM)
        wide = slice(i * group * HEAD_DIM, (i + 1) * group * HEAD_DIM)
        grad_query, grad_key, grad_value = add_terms(
            stacked_heads(q_ref, i * group, group), stacked_heads(do_ref, i * group, group),
            norm_row, delta_row, bias_ref[...], k_ref[:, at], v_ref[:, at], group,
        )
        dq_ref[:, wide] = grad_query
        dkv_ref[0, :, at] = grad_key
        dkv_ref[1, :, at] = grad_value


def halo_kernel(group, head_count, classes, split, *refs):
    q_ref, do_ref, norm_ref, delta_ref, start_ref, dq_in = refs[:6]
    at = 6
    kv = []
    for pair in split:
        if pair:
            kv.append((refs[at].at[0], refs[at + 1].at[0]))
            at += 2
        else:
            kv.append((refs[at].at[0], refs[at].at[1]))
            at += 1
    dq_ref = refs[at]
    outs = refs[at + 1 : at + 1 + len(classes)]
    bias_ref = refs[-1]
    g = pl.program_id(0)
    rows = q_ref.shape[0]

    @pl.when(g == 0)
    def _():
        c = lax.axis_index("ctx")
        p = lax.axis_index("head")
        key_at = lax.broadcasted_iota(jnp.int32, (rows, rows), 0)
        for i, m in enumerate(classes):
            source, plane = source_place(p, c, m)
            allowed = key_at + (plane * head_count + source) * rows >= start_ref[:1, :]
            bias_ref[i * rows : (i + 1) * rows, :] = jnp.where(allowed, 0.0, MASKED)

    for i in range(norm_ref.shape[0]):
        at = slice(i * HEAD_DIM, (i + 1) * HEAD_DIM)
        wide = slice(i * group * HEAD_DIM, (i + 1) * group * HEAD_DIM)
        grad_query, grad_key, grad_value = add_terms(
            stacked_heads(q_ref, i * group, group), stacked_heads(do_ref, i * group, group),
            norm_ref[i], delta_ref[i], bias_ref[...],
            jnp.concatenate([k[:, at] for k, _ in kv], axis=0),
            jnp.concatenate([v[:, at] for _, v in kv], axis=0),
            group,
        )
        dq_ref[:, wide] = (dq_in[:, wide] + grad_query).astype(dq_ref.dtype)
        for n, out in enumerate(outs):
            out[0, :, at] = grad_key[n * rows : (n + 1) * rows].astype(out.dtype)
            out[1, :, at] = grad_value[n * rows : (n + 1) * rows].astype(out.dtype)


def cost(blocks, rows, width):
    return pl.CostEstimate(
        flops=10 * blocks * rows * rows * width,
        bytes_accessed=8 * rows * width + blocks * rows * width,
        transcendentals=blocks * rows * rows * width // HEAD_DIM,
    )


def own_call(query, dout, out, norm, ids, key, value, head_count):
    rows, width = query.shape
    kv_heads = key.shape[1] // HEAD_DIM
    group = width // HEAD_DIM // kv_heads
    step = min(STEP_HEADS, kv_heads)
    wide = pl.BlockSpec((rows, step * group * HEAD_DIM), lambda g: (0, g))
    thin = pl.BlockSpec((rows, step * HEAD_DIM), lambda g: (0, g))
    whole = lambda a: pl.BlockSpec(a.shape, lambda g: (0,) * a.ndim)
    row = pl.BlockSpec((step, 1, group * rows), lambda g: (g, 0, 0))
    row_shape = jax.ShapeDtypeStruct((kv_heads, 1, group * rows), jnp.float32)
    return pl.pallas_call(
        functools.partial(own_kernel, group, head_count),
        grid=(kv_heads // step,),
        in_specs=[wide, wide, wide, whole(norm), whole(ids), thin, thin],
        out_specs=[
            wide,
            pl.BlockSpec((2, rows, step * HEAD_DIM), lambda g: (0, 0, g)),
            row,
            row,
            pl.BlockSpec((8, rows), lambda g: (0, 0)),
        ],
        out_shape=[
            jax.ShapeDtypeStruct((rows, width), jnp.float32),
            jax.ShapeDtypeStruct((2,) + key.shape, jnp.float32),
            row_shape,
            row_shape,
            jax.ShapeDtypeStruct((8, rows), jnp.int32),
        ],
        scratch_shapes=[
            pltpu.VMEM((rows, rows), jnp.float32),
            pltpu.VMEM((norm.shape[1], rows), jnp.float32),
        ],
        cost_estimate=cost(1, rows, width),
        name="own_block",
    )(query, dout, out, norm, ids, key, value)


def halo_call(query, dout, norms, deltas, starts, dq, classes, held, last, head_count):
    rows, width = query.shape
    kv_heads = norms.shape[0]
    group = width // HEAD_DIM // kv_heads
    step = min(STEP_HEADS, kv_heads)
    wide = pl.BlockSpec((rows, step * group * HEAD_DIM), lambda g: (0, g))
    row = pl.BlockSpec((step, 1, group * rows), lambda g: (g, 0, 0))
    pair = pl.BlockSpec((2, rows, step * HEAD_DIM), lambda g: (0, 0, g))
    single = pl.BlockSpec((1, rows, step * HEAD_DIM), lambda g: (0, 0, g))
    flat, specs, split = [], [], []
    for item in held:
        split.append(isinstance(item, tuple))
        for part in item if isinstance(item, tuple) else (item,):
            flat.append(part)
            specs.append(single if split[-1] else pair)
    out = jax.ShapeDtypeStruct((2, rows, kv_heads * HEAD_DIM), jnp.bfloat16)
    return pl.pallas_call(
        functools.partial(halo_kernel, group, head_count, tuple(classes), tuple(split)),
        grid=(kv_heads // step,),
        in_specs=[wide, wide, row, row, pl.BlockSpec((8, rows), lambda g: (0, 0)), wide] + specs,
        out_specs=[wide] + [pair] * len(classes),
        out_shape=[jax.ShapeDtypeStruct((rows, width), jnp.bfloat16 if last else jnp.float32)]
        + [out] * len(classes),
        scratch_shapes=[pltpu.VMEM((len(classes) * rows, rows), jnp.float32)],
        cost_estimate=cost(len(classes), rows, width),
        name="halo_blocks",
    )(query, dout, norms, deltas, starts, dq, *flat)


def solution(mesh):
    head_count = mesh.shape["head"]
    ctx_count = mesh.shape["ctx"]
    names = tuple(mesh.axis_names)

    def linear(c, p):
        at = {"head": p, "ctx": c}
        index = 0
        for name in names:
            index = index * mesh.shape[name] + at[name]
        return index

    places = [(c, p) for c in range(ctx_count) for p in range(head_count)]

    def later(c, p, m):
        if m == 0:
            return c + 1, p
        return c + (1 if (p ^ m) < p else 0), p ^ m

    def permute(value, moves):
        pairs = [(linear(*a), linear(*b)) for a, b in moves]
        return lax.ppermute(value, names, pairs)

    def inside(moves):
        return [(a, b) for a, b in moves if b[0] < ctx_count]

    def wrapped(place):
        return place[0] % ctx_count, place[1]

    def send(value, m):
        moves = [((c, p), later(c, p, m)) for c, p in places]
        moves = [(a, wrapped(b)) for a, b in moves] if m else inside(moves)
        return permute(value, moves)

    def send_back(value, m):
        moves = inside([((c, p), later(c, p, m)) for c, p in places])
        return permute(value, [(b, a) for a, b in moves])

    def relay(value, m, hop):
        moves = inside([(later(c, p, m ^ hop), later(c, p, m)) for c, p in places])
        return permute(value, [(wrapped(a), b) for a, b in moves])

    def local(query, key, value, out, dout, norm, doc_ids):
        rows = query.shape[0]
        kv = jnp.stack((key, value))
        singles = [m for m in range(1, head_count) if m & (m - 1) == 0]
        held = {m: send(kv, m) for m in singles + [0]}
        levels = [singles + [0]]
        for bits in range(2, head_count.bit_length()):
            level = [m for m in range(1, head_count) if bin(m).count("1") == bits]
            for m in level:
                low, high = m & -m, 1 << (m.bit_length() - 1)
                parts = []
                for side, hop in ((0, low), (1, high)):
                    via = held[m ^ hop]
                    part = via[side] if isinstance(via, tuple) else via[side : side + 1]
                    parts.append(relay(part, m, hop))
                held[m] = tuple(parts)
            levels.append(level)
        dq, own, norms, deltas, starts = own_call(
            query, dout, out, norm, doc_ids.reshape(-1, rows), key, value, head_count
        )
        back = []
        for i, level in enumerate(levels):
            dq, *terms = halo_call(
                query, dout, norms, deltas, starts, dq, level, [held[m] for m in level],
                i == len(levels) - 1, head_count,
            )
            back += [send_back(term, m) for term, m in zip(terms, level)]
        total = own
        for term in back:
            total = total + term.astype(jnp.float32)
        total = total.astype(jnp.bfloat16)
        return dq, total[0], total[1]

    spec = P(("ctx", "head"), None)
    return jax.shard_map(
        local,
        mesh=mesh,
        in_specs=(spec,) * 6 + (P(),),
        out_specs=(spec,) * 3,
        check_vma=False,
    )
```

time: 173 us -> 70.1 us (0.41)
  the two profiles are of different devices: /device:TPU:8 before, /device:TPU:0 now
where the time goes in v1:
time: 70.1 us; the launch traced here: 69.8 us
  waiting for transfers between devices  26 us (37%)
  starting transfers between devices  20.5 us (29%)
  Pallas kernels  18.6 us (27%)
  local copies, waits for them, and re-layouts  2.37 us (3%)
  other arithmetic  1.51 us (2%)
  between operations  0.78 us (1%)
    ppermute x9, waiting for transfers between devices, permute(): return lax.ppermute(value, names, pairs)  26 us
    ppermute x9, starting transfers between devices, permute(): return lax.ppermute(value, names, pairs)  20.5 us
    pallas_call x2, Pallas kernels, halo_call(): pl.pallas_call(functools.partial(halo_kernel, group, head_count, tuple(cl...  13.1 us
    pallas_call x1, Pallas kernels, own_call(): pl.pallas_call(functools.partial(own_kernel, group, head_count), grid=(kv...  5.56 us
    unnamed x13, local copies, waits for them, and re-layouts  1.51 us
  transfers between devices with their start and end apart: 9, of which 5 were waited for; matrix products, arithmetic and copies ran while one was open for 1% of the time, Pallas kernels for 27%

profile of v1, /device:TPU:0, one launch (start us, length us, event | category | flops | bytes accessed | tf_op | source)
XLA Modules:
  0.0 69.8 jit_solution(14518556716891414510)
XLA Ops:
  0.6 0.0 copy-start.5
  0.6 1.1 %pad_maximum_fusion = bf16[2,128,1024]{2,1,0:T(8,128)(2,1)S(1)} fusion(bf16[1,128,1024]{2,1,0:T(8,128)(2,1)} %bitcast.8, bf16[1,128,1024]{2,1,0:T(8,128)(2,1)} %bitcast.7), kind=kLoop, calls=%fused_computation.1 | loop fusion | flops 262144 | bytes 1048576 | tf_op jit(solution)/shard_map/stack | solution.py:263
  1.7 3.1 %collective-permute-start.1 = (bf16[2,128,1024]{2,1,0:T(8,128)(2,1)S(1)}, bf16[2,128,1024]{2,1,0:T(8,128)(2,1)S(1)}, u32[]{:S(2)}, u32[]{:S(2)}) collective-permute-start(bf16[2,128,1024]{2,1,0:T(8,128)(2,1)S(1)} %pad_maximum_fusion), channel_id=1, source_target_pairs={{0,16},{8,24},{16,1},{24,9},{1,17},{9,25},{17,2},{25,10},{2,18},{1... | collective-permute-start | bytes 1572872 | tf_op jit(solution)/shard_map/ppermute | solution.py:240
  4.8 1.5 %collective-permute-start = (bf16[2,128,1024]{2,1,0:T(8,128)(2,1)S(1)}, bf16[2,128,1024]{2,1,0:T(8,128)(2,1)S(1)}, u32[]{:S(2)}, u32[]{:S(2)}) collective-permute-start(bf16[2,128,1024]{2,1,0:T(8,128)(2,1)S(1)} %pad_maximum_fusion), channel_id=1, source_target_pairs={{0,8},{8,1},{16,24},{24,17},{1,9},{9,2},{17,25},{25,18},{2,10},{10... | collective-permute-start | bytes 1572872 | tf_op jit(solution)/shard_map/ppermute | solution.py:240
  6.3 2.1 %collective-permute-start.2 = (bf16[2,128,1024]{2,1,0:T(8,128)(2,1)S(1)}, bf16[2,128,1024]{2,1,0:T(8,128)(2,1)}, u32[]{:S(2)}, u32[]{:S(2)}) collective-permute-start(bf16[2,128,1024]{2,1,0:T(8,128)(2,1)S(1)} %pad_maximum_fusion), channel_id=1, source_target_pairs={{0,1},{8,9},{16,17},{24,25},{1,2},{9,10},{17,18},{25,26},{2,3},{10... | collective-permute-start | bytes 1572872 | tf_op jit(solution)/shard_map/ppermute | solution.py:240
  8.4 7.6 %collective-permute-done.1.refs_7_ = bf16[2,128,1024]{2,1,0:T(8,128)(2,1)S(1)} collective-permute-done((bf16[2,128,1024]{2,1,0:T(8,128)(2,1)S(1)}, bf16[2,128,1024]{2,1,0:T(8,128)(2,1)S(1)}, u32[]{:S(2)}, u32[]{:S(2)}) %collective-permute-start.1) | collective-permute-done | bytes 524320 | tf_op jit(solution)/shard_map/ppermute | solution.py:240
  16.0 0.7 collective-permute-start.3
  16.7 0.5 collective-permute-done.refs_6_
  17.2 8.0 %collective-permute-start.4 = (bf16[1,128,1024]{2,1,0:T(8,128)(2,1)S(1)}, bf16[1,128,1024]{2,1,0:T(8,128)(2,1)S(1)}, u32[]{:S(2)}, u32[]{:S(2)}) collective-permute-start(bf16[1,128,1024]{2,1,0:T(8,128)(2,1)S(1)} %slice.17), channel_id=1, source_target_pairs={{8,24},{1,16},{24,9},{17,1},{9,25},{2,17},{25,10},{18,2},{10,26},{... | collective-permute-start | bytes 786440 | tf_op jit(solution)/shard_map/ppermute | solution.py:240
  25.2 0.7 %copy.10.norm_ref = f32[128,32]{1,0:T(8,128)} copy(f32[128,32]{0,1:T(8,128)S(1)} %copy-done.5) | data formatting | bytes 32768 | tf_op args[5]
  25.9 5.6 %own_block.1 = (f32[128,4096]{1,0:T(8,128)}, f32[2,128,1024]{2,1,0:T(8,128)}, f32[8,1,512]{2,1,0:T(1,128)}, f32[8,1,512]{2,1,0:T(1,128)}, s32[8,128]{1,0:T(8,128)}) custom-call(bf16[128,4096]{1,0:T(8,128)(2,1)} %refs_0_.3, bf16[128,4096]{1,0:T(8,128)(2,1)} %refs_1_.3, bf16[128,4096]{1,0:T(8,128)(2,1)} %o_ref.1, f32[128,32]{1,0:T(8,128)} %copy.10.norm_ref, ...), custom_call_target="tpu_custom_call" | custom-call | flops 671088640 | bytes 4718592 | tf_op jit(solution)/shard_map/own_block/pallas_call | solution.py:163
  31.5 0.0 copy-done.3
  31.5 0.0 copy-done.4
  31.5 0.0 collective-permute-done.2.refs_8_
  31.5 7.8 %halo_blocks.2 = (f32[128,4096]{1,0:T(8,128)}, bf16[2,128,1024]{2,1,0:T(8,128)(2,1)}, bf16[2,128,1024]{2,1,0:T(8,128)(2,1)}, bf16[2,128,1024]{2,1,0:T(8,128)(2,1)}) custom-call(bf16[128,4096]{1,0:T(8,128)(2,1)} %refs_0_.3, bf16[128,4096]{1,0:T(8,128)(2,1)} %refs_1_.3, f32[8,1,512]{2,1,0:T(1,128)} %get-tuple-element.14.refs_2_, ...), custom_call_target="tpu_custom_call" | custom-call | flops 2013265920 | bytes 5767168 | tf_op jit(solution)/shard_map/halo_blocks/pallas_call | solution.py:206
  39.4 1.3 %collective-permute-start.5 = (bf16[2,128,1024]{2,1,0:T(8,128)(2,1)}, bf16[2,128,1024]{2,1,0:T(8,128)(2,1)S(1)}, u32[]{:S(2)}, u32[]{:S(2)}) collective-permute-start(bf16[2,128,1024]{2,1,0:T(8,128)(2,1)} %get-tuple-element.21), channel_id=1, source_target_pairs={{8,0},{1,8},{24,16},{17,24},{9,1},{2,9},{25,17},{18,25},{10,2},{3,... | collective-permute-start | bytes 1572872 | tf_op jit(solution)/shard_map/ppermute | solution.py:240
  40.7 1.3 %collective-permute-start.6 = (bf16[2,128,1024]{2,1,0:T(8,128)(2,1)}, bf16[2,128,1024]{2,1,0:T(8,128)(2,1)S(1)}, u32[]{:S(2)}, u32[]{:S(2)}) collective-permute-start(bf16[2,128,1024]{2,1,0:T(8,128)(2,1)} %get-tuple-element.22), channel_id=1, source_target_pairs={{16,0},{24,8},{1,16},{9,24},{17,1},{25,9},{2,17},{10,25},{18,2},{2... | collective-permute-start | bytes 1572872 | tf_op jit(solution)/shard_map/ppermute | solution.py:240
  42.0 1.3 %collective-permute-start.7 = (bf16[2,128,1024]{2,1,0:T(8,128)(2,1)}, bf16[2,128,1024]{2,1,0:T(8,128)(2,1)S(1)}, u32[]{:S(2)}, u32[]{:S(2)}) collective-permute-start(bf16[2,128,1024]{2,1,0:T(8,128)(2,1)} %get-tuple-element.23), channel_id=1, source_target_pairs={{1,0},{9,8},{17,16},{25,24},{2,1},{10,9},{18,17},{26,25},{3,2},{11... | collective-permute-start | bytes 1572872 | tf_op jit(solution)/shard_map/ppermute | solution.py:240
  43.3 0.0 collective-permute-done.3.refs_6_
  43.3 0.0 copy-start.1
  43.3 0.0 collective-permute-done.4.refs_7_
  43.3 0.0 copy-start.2
  43.3 0.7 copy-done.1
  44.0 0.1 copy-done.2
  44.1 5.3 %halo_blocks.3 = (bf16[128,4096]{1,0:T(8,128)(2,1)}, bf16[2,128,1024]{2,1,0:T(8,128)(2,1)}) custom-call(bf16[128,4096]{1,0:T(8,128)(2,1)} %refs_0_.3, bf16[128,4096]{1,0:T(8,128)(2,1)} %refs_1_.3, f32[8,1,512]{2,1,0:T(1,128)} %get-tuple-element.14.refs_2_, f32[8,1,512]{2,1,0:T(1,128)} %get-tuple-element.15.refs_3_, s32[8,128]{1,0:T(8,128)} %get-tuple-element.16.refs_4_, ...), custom_call_target="tpu_custom_call" | custom-call | flops 671088640 | bytes 4718592 | tf_op jit(solution)/shard_map/halo_blocks/pallas_call | solution.py:206
  49.3 1.3 %collective-permute-start.8 = (bf16[2,128,1024]{2,1,0:T(8,128)(2,1)}, bf16[2,128,1024]{2,1,0:T(8,128)(2,1)S(1)}, u32[]{:S(2)}, u32[]{:S(2)}) collective-permute-start(bf16[2,128,1024]{2,1,0:T(8,128)(2,1)} %get-tuple-element.24), channel_id=1, source_target_pairs={{24,0},{16,8},{9,16},{1,24},{25,1},{17,9},{10,17},{2,25},{26,2},{1... | collective-permute-start | bytes 1572872 | tf_op jit(solution)/shard_map/ppermute | solution.py:240
  50.6 3.5 %collective-permute-done.5 = bf16[2,128,1024]{2,1,0:T(8,128)(2,1)S(1)} collective-permute-done((bf16[2,128,1024]{2,1,0:T(8,128)(2,1)}, bf16[2,128,1024]{2,1,0:T(8,128)(2,1)S(1)}, u32[]{:S(2)}, u32[]{:S(2)}) %collective-permute-start.5) | collective-permute-done | bytes 524320 | tf_op jit(solution)/shard_map/ppermute | solution.py:240
  54.1 2.5 %collective-permute-done.6 = bf16[2,128,1024]{2,1,0:T(8,128)(2,1)S(1)} collective-permute-done((bf16[2,128,1024]{2,1,0:T(8,128)(2,1)}, bf16[2,128,1024]{2,1,0:T(8,128)(2,1)S(1)}, u32[]{:S(2)}, u32[]{:S(2)}) %collective-permute-start.6) | collective-permute-done | bytes 524320 | tf_op jit(solution)/shard_map/ppermute | solution.py:240
  56.5 0.0 collective-permute-done.7
  56.5 12.0 %collective-permute-done.8 = bf16[2,128,1024]{2,1,0:T(8,128)(2,1)S(1)} collective-permute-done((bf16[2,128,1024]{2,1,0:T(8,128)(2,1)}, bf16[2,128,1024]{2,1,0:T(8,128)(2,1)S(1)}, u32[]{:S(2)}, u32[]{:S(2)}) %collective-permute-start.8) | collective-permute-done | bytes 524320 | tf_op jit(solution)/shard_map/ppermute | solution.py:240
  68.5 0.4 add_convert_fusion
  68.9 0.8 %slice_bitcast_fusion = (bf16[128,1024]{1,0:T(8,128)(2,1)}, bf16[128,1024]{1,0:T(8,128)(2,1)}) fusion(bf16[2,128,1024]{2,1,0:T(8,128)(2,1)S(1)} %add_convert_fusion), kind=kLoop, calls=%fused_computation.2 | loop fusion | bytes 1048576 | tf_op jit(solution)/shard_map/squeeze | solution.py:292
  (7 shorter events, 0.0 us)
Async XLA Ops:
  0.6 24.6 %copy-start.5 = (f32[128,32]{0,1:T(8,128)S(1)}, f32[128,32]{0,1:T(8,128)}, u32[]{:S(2)}) copy-start(f32[128,32]{0,1:T(8,128)} %param.12) | copy-start | bytes 49156
  1.7 14.2 %collective-permute-start.1 = (bf16[2,128,1024]{2,1,0:T(8,128)(2,1)S(1)}, bf16[2,128,1024]{2,1,0:T(8,128)(2,1)S(1)}, u32[]{:S(2)}, u32[]{:S(2)}) collective-permute-start(bf16[2,128,1024]{2,1,0:T(8,128)(2,1)S(1)} %pad_maximum_fusion), channel_id=1, source_target_pairs={{0,16},{8,24},{16,1},{24,9},{1,17},{9,25},{17,2},{25,10},{2,18},{1... | collective-permute-start | bytes 1572872 | tf_op jit(solution)/shard_map/ppermute | solution.py:240
  4.8 12.4 %collective-permute-start = (bf16[2,128,1024]{2,1,0:T(8,128)(2,1)S(1)}, bf16[2,128,1024]{2,1,0:T(8,128)(2,1)S(1)}, u32[]{:S(2)}, u32[]{:S(2)}) collective-permute-start(bf16[2,128,1024]{2,1,0:T(8,128)(2,1)S(1)} %pad_maximum_fusion), channel_id=1, source_target_pairs={{0,8},{8,1},{16,24},{24,17},{1,9},{9,2},{17,25},{25,18},{2,10},{10... | collective-permute-start | bytes 1572872 | tf_op jit(solution)/shard_map/ppermute | solution.py:240
  6.3 25.3 %collective-permute-start.2 = (bf16[2,128,1024]{2,1,0:T(8,128)(2,1)S(1)}, bf16[2,128,1024]{2,1,0:T(8,128)(2,1)}, u32[]{:S(2)}, u32[]{:S(2)}) collective-permute-start(bf16[2,128,1024]{2,1,0:T(8,128)(2,1)S(1)} %pad_maximum_fusion), channel_id=1, source_target_pairs={{0,1},{8,9},{16,17},{24,25},{1,2},{9,10},{17,18},{25,26},{2,3},{10... | collective-permute-start | bytes 1572872 | tf_op jit(solution)/shard_map/ppermute | solution.py:240
  16.0 15.5 %copy-start.3 = (bf16[2,128,1024]{2,1,0:T(8,128)(2,1)}, bf16[2,128,1024]{2,1,0:T(8,128)(2,1)S(1)}, u32[]{:S(2)}) copy-start(bf16[2,128,1024]{2,1,0:T(8,128)(2,1)S(1)} %collective-permute-done.1.refs_7_) | copy-start | bytes 1572868
  16.0 27.3 %collective-permute-start.3 = (bf16[1,128,1024]{2,1,0:T(8,128)(2,1)S(1)}, bf16[1,128,1024]{2,1,0:T(8,128)(2,1)S(1)}, u32[]{:S(2)}, u32[]{:S(2)}) collective-permute-start(bf16[1,128,1024]{2,1,0:T(8,128)(2,1)S(1)} %slice.16), channel_id=1, source_target_pairs={{16,24},{24,16},{1,9},{9,1},{17,25},{25,17},{2,10},{10,2},{18,26},... | collective-permute-start | bytes 786440 | tf_op jit(solution)/shard_map/ppermute | solution.py:240
  17.2 14.3 %copy-start.4 = (bf16[2,128,1024]{2,1,0:T(8,128)(2,1)}, bf16[2,128,1024]{2,1,0:T(8,128)(2,1)S(1)}, u32[]{:S(2)}) copy-start(bf16[2,128,1024]{2,1,0:T(8,128)(2,1)S(1)} %collective-permute-done.refs_6_) | copy-start | bytes 1572868
  17.2 26.1 %collective-permute-start.4 = (bf16[1,128,1024]{2,1,0:T(8,128)(2,1)S(1)}, bf16[1,128,1024]{2,1,0:T(8,128)(2,1)S(1)}, u32[]{:S(2)}, u32[]{:S(2)}) collective-permute-start(bf16[1,128,1024]{2,1,0:T(8,128)(2,1)S(1)} %slice.17), channel_id=1, source_target_pairs={{8,24},{1,16},{24,9},{17,1},{9,25},{2,17},{25,10},{18,2},{10,26},{... | collective-permute-start | bytes 786440 | tf_op jit(solution)/shard_map/ppermute | solution.py:240
  39.4 14.7 %collective-permute-start.5 = (bf16[2,128,1024]{2,1,0:T(8,128)(2,1)}, bf16[2,128,1024]{2,1,0:T(8,128)(2,1)S(1)}, u32[]{:S(2)}, u32[]{:S(2)}) collective-permute-start(bf16[2,128,1024]{2,1,0:T(8,128)(2,1)} %get-tuple-element.21), channel_id=1, source_target_pairs={{8,0},{1,8},{24,16},{17,24},{9,1},{2,9},{25,17},{18,25},{10,2},{3,... | collective-permute-start | bytes 1572872 | tf_op jit(solution)/shard_map/ppermute | solution.py:240
  40.7 15.9 %collective-permute-start.6 = (bf16[2,128,1024]{2,1,0:T(8,128)(2,1)}, bf16[2,128,1024]{2,1,0:T(8,128)(2,1)S(1)}, u32[]{:S(2)}, u32[]{:S(2)}) collective-permute-start(bf16[2,128,1024]{2,1,0:T(8,128)(2,1)} %get-tuple-element.22), channel_id=1, source_target_pairs={{16,0},{24,8},{1,16},{9,24},{17,1},{25,9},{2,17},{10,25},{18,2},{2... | collective-permute-start | bytes 1572872 | tf_op jit(solution)/shard_map/ppermute | solution.py:240
  42.0 14.6 %collective-permute-start.7 = (bf16[2,128,1024]{2,1,0:T(8,128)(2,1)}, bf16[2,128,1024]{2,1,0:T(8,128)(2,1)S(1)}, u32[]{:S(2)}, u32[]{:S(2)}) collective-permute-start(bf16[2,128,1024]{2,1,0:T(8,128)(2,1)} %get-tuple-element.23), channel_id=1, source_target_pairs={{1,0},{9,8},{17,16},{25,24},{2,1},{10,9},{18,17},{26,25},{3,2},{11... | collective-permute-start | bytes 1572872 | tf_op jit(solution)/shard_map/ppermute | solution.py:240
  43.3 0.7 %copy-start.1 = (bf16[1,128,1024]{2,1,0:T(8,128)(2,1)}, bf16[1,128,1024]{2,1,0:T(8,128)(2,1)S(1)}, u32[]{:S(2)}) copy-start(bf16[1,128,1024]{2,1,0:T(8,128)(2,1)S(1)} %collective-permute-done.3.refs_6_) | copy-start | bytes 786436
  43.3 0.8 %copy-start.2 = (bf16[1,128,1024]{2,1,0:T(8,128)(2,1)}, bf16[1,128,1024]{2,1,0:T(8,128)(2,1)S(1)}, u32[]{:S(2)}) copy-start(bf16[1,128,1024]{2,1,0:T(8,128)(2,1)S(1)} %collective-permute-done.4.refs_7_) | copy-start | bytes 786436
  44.1 24.4 %copy-start = (f32[2,128,1024]{2,1,0:T(8,128)S(1)}, f32[2,128,1024]{2,1,0:T(8,128)}, u32[]{:S(2)}) copy-start(f32[2,128,1024]{2,1,0:T(8,128)} %get-tuple-element.20) | copy-start | bytes 3145732
  49.3 19.2 %collective-permute-start.8 = (bf16[2,128,1024]{2,1,0:T(8,128)(2,1)}, bf16[2,128,1024]{2,1,0:T(8,128)(2,1)S(1)}, u32[]{:S(2)}, u32[]{:S(2)}) collective-permute-start(bf16[2,128,1024]{2,1,0:T(8,128)(2,1)} %get-tuple-element.24), channel_id=1, source_target_pairs={{24,0},{16,8},{9,16},{1,24},{25,1},{17,9},{10,17},{2,25},{26,2},{1... | collective-permute-start | bytes 1572872 | tf_op jit(solution)/shard_map/ppermute | solution.py:240

commit v2 on v1

--- a/solution.py
+++ b/solution.py
@@ -7,8 +7,10 @@
 from jax.experimental.pallas import tpu as pltpu
 from jax.sharding import PartitionSpec as P
 
+
 HEAD_DIM = 128
 MASKED = -1e30
+VMEM_LIMIT = 24 << 20
 STEP_HEADS = 4
 NT = (((1,), (1,)), ((), ()))
 NN = (((1,), (0,)), ((), ()))
@@ -183,6 +185,7 @@
             pltpu.VMEM((norm.shape[1], rows), jnp.float32),
         ],
         cost_estimate=cost(1, rows, width),
+        compiler_params=pltpu.CompilerParams(vmem_limit_bytes=VMEM_LIMIT),
         name="own_block",
     )(query, dout, out, norm, ids, key, value)
 
@@ -212,6 +215,7 @@
         + [out] * len(classes),
         scratch_shapes=[pltpu.VMEM((len(classes) * rows, rows), jnp.float32)],
         cost_estimate=cost(len(classes), rows, width),
+        compiler_params=pltpu.CompilerParams(vmem_limit_bytes=VMEM_LIMIT),
         name="halo_blocks",
     )(query, dout, norms, deltas, starts, dq, *flat)
 
@@ -236,27 +240,19 @@
         return c + (1 if (p ^ m) < p else 0), p ^ m
 
     def permute(value, moves):
-        pairs = [(linear(*a), linear(*b)) for a, b in moves]
+        pairs = []
+        for (c, p), (c2, p2) in moves:
+            pairs.append((linear(c % ctx_count, p), linear(c2 % ctx_count, p2)))
         return lax.ppermute(value, names, pairs)
 
-    def inside(moves):
-        return [(a, b) for a, b in moves if b[0] < ctx_count]
-
-    def wrapped(place):
-        return place[0] % ctx_count, place[1]
-
     def send(value, m):
-        moves = [((c, p), later(c, p, m)) for c, p in places]
-        moves = [(a, wrapped(b)) for a, b in moves] if m else inside(moves)
-        return permute(value, moves)
+        return permute(value, [((c, p), later(c, p, m)) for c, p in places])
 
     def send_back(value, m):
-        moves = inside([((c, p), later(c, p, m)) for c, p in places])
-        return permute(value, [(b, a) for a, b in moves])
+        return permute(value, [(later(c, p, m), (c, p)) for c, p in places])
 
     def relay(value, m, hop):
-        moves = inside([(later(c, p, m ^ hop), later(c, p, m)) for c, p in places])
-        return permute(value, [(wrapped(a), b) for a, b in moves])
+        return permute(value, [(later(c, p, m ^ hop), later(c, p, m)) for c, p in places])
 
     def local(query, key, value, out, dout, norm, doc_ids):
         rows = query.shape[0]

time: 70.1 us -> 63.4 us (0.904)
  Pallas kernels: 18.6 us -> 13.4 us
  starting transfers between devices: 20.5 us -> 15.8 us
  local copies, waits for them, and re-layouts: 2.37 us -> 4.98 us
  other arithmetic: 1.51 us -> 2.44 us
    ppermute x9, starting transfers between devices: 20.5 us -> 15.8 us  [permute(): return lax.ppermute(value, names, pairs)]
    pallas_call x2, Pallas kernels: 13.1 us -> 10 us  [halo_call(): pl.pallas_call(functools.partial(halo_kernel, group, head_count, tuple(cl...]
    pallas_call x1, Pallas kernels: 5.56 us -> 3.34 us  [own_call(): pl.pallas_call(functools.partial(own_kernel, group, head_count), grid=(kv...]
    unnamed x13 -> x19, local copies, waits for them, and re-layouts: 1.51 us -> 3.38 us
    another operation x1, other arithmetic: 1.08 us -> 2.02 us  [local(): kv = jnp.stack((key, value))]
    slice x2, local copies, waits for them, and re-layouts: 0.04 us -> 0.78 us  [local(): part = via[side] if isinstance(via, tuple) else via[side:side + 1]]
  transfers between devices with their start and end apart: 9 -> 9, of which waited for: 5 -> 3; matrix products, arithmetic and copies ran while one was open for 1% -> 1% of each run, Pallas kernels for 27% -> 21%
where the time goes in v2:
time: 63.4 us; the launch traced here: 63.2 us
  waiting for transfers between devices  25.8 us (41%)
  starting transfers between devices  15.8 us (25%)
  Pallas kernels  13.4 us (21%)
  local copies, waits for them, and re-layouts  4.98 us (8%)
  other arithmetic  2.44 us (4%)
  between operations  0.75 us (1%)
    ppermute x9, waiting for transfers between devices, permute(): return lax.ppermute(value, names, pairs)  25.8 us
    ppermute x9, starting transfers between devices, permute(): return lax.ppermute(value, names, pairs)  15.8 us
    pallas_call x2, Pallas kernels, halo_call(): pl.pallas_call(functools.partial(halo_kernel, group, head_count, tuple(cl...  10 us
    unnamed x19, local copies, waits for them, and re-layouts  3.38 us
    pallas_call x1, Pallas kernels, own_call(): pl.pallas_call(functools.partial(own_kernel, group, head_count), grid=(kv...  3.34 us
    another operation x1, other arithmetic, local(): kv = jnp.stack((key, value))  2.02 us
  transfers between devices with their start and end apart: 9, of which 3 were waited for; matrix products, arithmetic and copies ran while one was open for 1% of the time, Pallas kernels for 21%

profile of v2, /device:TPU:0, one launch (start us, length us, event | category | flops | bytes accessed | tf_op | source)
XLA Modules:
  0.0 63.2 jit_solution(11001533568385044973)
XLA Ops:
  0.6 0.0 copy-start.8
  0.7 2.0 %pad_maximum_fusion = bf16[2,128,1024]{2,1,0:T(8,128)(2,1)} fusion(bf16[1,128,1024]{2,1,0:T(8,128)(2,1)} %bitcast.8, bf16[1,128,1024]{2,1,0:T(8,128)(2,1)} %bitcast.7), kind=kLoop, calls=%fused_computation.1 | loop fusion | flops 262144 | bytes 1048576 | tf_op jit(solution)/shard_map/stack | solution.py:259
  2.7 3.0 %collective-permute-start.1 = (bf16[2,128,1024]{2,1,0:T(8,128)(2,1)}, bf16[2,128,1024]{2,1,0:T(8,128)(2,1)S(1)}, u32[]{:S(2)}, u32[]{:S(2)}) collective-permute-start(bf16[2,128,1024]{2,1,0:T(8,128)(2,1)} %pad_maximum_fusion), channel_id=1, source_target_pairs={{0,16},{8,24},{16,1},{24,9},{1,17},{9,25},{17,2},{25,10},{2,18},{1... | collective-permute-start | bytes 1572872 | tf_op jit(solution)/shard_map/ppermute | solution.py:246
  5.7 1.5 %collective-permute-start = (bf16[2,128,1024]{2,1,0:T(8,128)(2,1)}, bf16[2,128,1024]{2,1,0:T(8,128)(2,1)S(1)}, u32[]{:S(2)}, u32[]{:S(2)}) collective-permute-start(bf16[2,128,1024]{2,1,0:T(8,128)(2,1)} %pad_maximum_fusion), channel_id=1, source_target_pairs={{0,8},{8,1},{16,24},{24,17},{1,9},{9,2},{17,25},{25,18},{2,10},{10... | collective-permute-start | bytes 1572872 | tf_op jit(solution)/shard_map/ppermute | solution.py:246
  7.2 0.0 collective-permute-start.2
  7.2 10.0 %collective-permute-done.1.refs_7_ = bf16[2,128,1024]{2,1,0:T(8,128)(2,1)S(1)} collective-permute-done((bf16[2,128,1024]{2,1,0:T(8,128)(2,1)}, bf16[2,128,1024]{2,1,0:T(8,128)(2,1)S(1)}, u32[]{:S(2)}, u32[]{:S(2)}) %collective-permute-start.1) | collective-permute-done | bytes 524320 | tf_op jit(solution)/shard_map/ppermute | solution.py:246
  17.2 1.6 %collective-permute-start.3 = (bf16[1,128,1024]{2,1,0:T(8,128)(2,1)S(1)}, bf16[1,128,1024]{2,1,0:T(8,128)(2,1)S(1)}, u32[]{:S(2)}, u32[]{:S(2)}) collective-permute-start(bf16[1,128,1024]{2,1,0:T(8,128)(2,1)S(1)} %slice.16), channel_id=1, source_target_pairs={{16,24},{24,16},{1,9},{9,1},{17,25},{25,17},{2,10},{10,2},{18,26},... | collective-permute-start | bytes 786440 | tf_op jit(solution)/shard_map/ppermute | solution.py:246
  18.8 0.0 collective-permute-done.refs_6_
  18.8 0.8 %slice.17 = bf16[1,128,1024]{2,1,0:T(8,128)(2,1)} slice(bf16[2,128,1024]{2,1,0:T(8,128)(2,1)S(1)} %collective-permute-done.refs_6_), slice={[1:2], [0:128], [0:1024]} | slice | bytes 524288 | tf_op jit(solution)/shard_map/slice | solution.py:270
  19.5 0.1 copy-done.5
  19.7 3.7 %collective-permute-start.4 = (bf16[1,128,1024]{2,1,0:T(8,128)(2,1)}, bf16[1,128,1024]{2,1,0:T(8,128)(2,1)S(1)}, u32[]{:S(2)}, u32[]{:S(2)}) collective-permute-start(bf16[1,128,1024]{2,1,0:T(8,128)(2,1)} %slice.17), channel_id=1, source_target_pairs={{8,24},{1,16},{24,9},{17,1},{9,25},{2,17},{25,10},{18,2},{10,26},{... | collective-permute-start | bytes 786440 | tf_op jit(solution)/shard_map/ppermute | solution.py:246
  23.4 0.1 copy.10.norm_ref
  23.5 0.0 copy-start.2
  23.5 0.9 %copy-done.2 = bf16[128,1024]{1,0:T(8,128)(2,1)S(1)} copy-done((bf16[128,1024]{1,0:T(8,128)(2,1)S(1)}, bf16[128,1024]{1,0:T(8,128)(2,1)}, u32[]{:S(2)}) %copy-start.2) | copy-done | bytes 262168
  24.5 0.9 %copy-done.3 = bf16[128,1024]{1,0:T(8,128)(2,1)S(1)} copy-done((bf16[128,1024]{1,0:T(8,128)(2,1)S(1)}, bf16[128,1024]{1,0:T(8,128)(2,1)}, u32[]{:S(2)}) %copy-start.3) | copy-done | bytes 262168
  25.4 1.2 %copy-done.4 = bf16[128,4096]{1,0:T(8,128)(2,1)S(1)} copy-done((bf16[128,4096]{1,0:T(8,128)(2,1)S(1)}, bf16[128,4096]{1,0:T(8,128)(2,1)}, u32[]{:S(2)}) %copy-start.4) | copy-done | bytes 1048600
  26.6 3.3 %own_block.1 = (f32[128,4096]{1,0:T(8,128)S(1)}, f32[2,128,1024]{2,1,0:T(8,128)S(1)}, f32[8,1,512]{2,1,0:T(1,128)S(1)}, f32[8,1,512]{2,1,0:T(1,128)S(1)}, s32[8,128]{1,0:T(8,128)S(1)}) custom-call(bf16[128,4096]{1,0:T(8,128)(2,1)S(1)} %copy-done, bf16[128,4096]{1,0:T(8,128)(2,1)S(1)} %copy-done.1, bf16[128,4096]{1,0:T(8,128)(2,1)S(1)} %copy-done.4, ...), custom_call_target="tpu_custom_call" | custom-call | flops 671088640 | bytes 4718592 | tf_op jit(solution)/shard_map/own_block/pallas_call | solution.py:165
  30.0 0.0 collective-permute-done.2.refs_8_
  30.0 6.1 %halo_blocks.2 = (f32[128,4096]{1,0:T(8,128)S(1)}, bf16[2,128,1024]{2,1,0:T(8,128)(2,1)S(1)}, bf16[2,128,1024]{2,1,0:T(8,128)(2,1)S(1)}, bf16[2,128,1024]{2,1,0:T(8,128)(2,1)S(1)}) custom-call(bf16[128,4096]{1,0:T(8,128)(2,1)S(1)} %copy-done, bf16[128,4096]{1,0:T(8,128)(2,1)S(1)} %copy-done.1, f32[8,1,512]{2,1,0:T(1,128)S(1)} %get-tuple-element.14.refs_2_, ...), custom_call_target="tpu_custom_call" | custom-call | flops 2013265920 | bytes 5767168 | tf_op jit(solution)/shard_map/halo_blocks/pallas_call | solution.py:209
  36.2 0.9 %collective-permute-start.5 = (bf16[2,128,1024]{2,1,0:T(8,128)(2,1)S(1)}, bf16[2,128,1024]{2,1,0:T(8,128)(2,1)S(1)}, u32[]{:S(2)}, u32[]{:S(2)}) collective-permute-start(bf16[2,128,1024]{2,1,0:T(8,128)(2,1)S(1)} %get-tuple-element.21), channel_id=1, source_target_pairs={{8,0},{1,8},{24,16},{17,24},{9,1},{2,9},{25,17},{18,25},{10,2},{3,... | collective-permute-start | bytes 1572872 | tf_op jit(solution)/shard_map/ppermute | solution.py:246
  37.0 1.6 %collective-permute-start.6 = (bf16[2,128,1024]{2,1,0:T(8,128)(2,1)S(1)}, bf16[2,128,1024]{2,1,0:T(8,128)(2,1)S(1)}, u32[]{:S(2)}, u32[]{:S(2)}) collective-permute-start(bf16[2,128,1024]{2,1,0:T(8,128)(2,1)S(1)} %get-tuple-element.22), channel_id=1, source_target_pairs={{16,0},{24,8},{1,16},{9,24},{17,1},{25,9},{2,17},{10,25},{18,2},{2... | collective-permute-start | bytes 1572872 | tf_op jit(solution)/shard_map/ppermute | solution.py:246
  38.6 1.9 %collective-permute-start.7 = (bf16[2,128,1024]{2,1,0:T(8,128)(2,1)S(1)}, bf16[2,128,1024]{2,1,0:T(8,128)(2,1)S(1)}, u32[]{:S(2)}, u32[]{:S(2)}) collective-permute-start(bf16[2,128,1024]{2,1,0:T(8,128)(2,1)S(1)} %get-tuple-element.23), channel_id=1, source_target_pairs={{1,0},{9,8},{17,16},{25,24},{2,1},{10,9},{18,17},{26,25},{3,2},{11... | collective-permute-start | bytes 1572872 | tf_op jit(solution)/shard_map/ppermute | solution.py:246
  40.5 0.0 collective-permute-done.3.refs_6_
  40.5 0.0 collective-permute-done.4.refs_7_
  40.5 3.9 %halo_blocks.3 = (bf16[128,4096]{1,0:T(8,128)(2,1)}, bf16[2,128,1024]{2,1,0:T(8,128)(2,1)S(1)}) custom-call(bf16[128,4096]{1,0:T(8,128)(2,1)S(1)} %copy-done, bf16[128,4096]{1,0:T(8,128)(2,1)S(1)} %copy-done.1, f32[8,1,512]{2,1,0:T(1,128)S(1)} %get-tuple-element.14.refs_2_, f32[8,1,512]{2,1,0:T(1,128)S(1)} %get-tuple-element.15.refs_3_, ...), custom_call_target="tpu_custom_call" | custom-call | flops 671088640 | bytes 4718592 | tf_op jit(solution)/shard_map/halo_blocks/pallas_call | solution.py:209
  44.4 1.7 %collective-permute-start.8 = (bf16[2,128,1024]{2,1,0:T(8,128)(2,1)S(1)}, bf16[2,128,1024]{2,1,0:T(8,128)(2,1)S(1)}, u32[]{:S(2)}, u32[]{:S(2)}) collective-permute-start(bf16[2,128,1024]{2,1,0:T(8,128)(2,1)S(1)} %get-tuple-element.24), channel_id=1, source_target_pairs={{24,0},{16,8},{9,16},{1,24},{25,1},{17,9},{10,17},{2,25},{26,2},{1... | collective-permute-start | bytes 1572872 | tf_op jit(solution)/shard_map/ppermute | solution.py:246
  46.1 4.9 %collective-permute-done.5 = bf16[2,128,1024]{2,1,0:T(8,128)(2,1)S(1)} collective-permute-done((bf16[2,128,1024]{2,1,0:T(8,128)(2,1)S(1)}, bf16[2,128,1024]{2,1,0:T(8,128)(2,1)S(1)}, u32[]{:S(2)}, u32[]{:S(2)}) %collective-permute-start.5) | collective-permute-done | bytes 524320 | tf_op jit(solution)/shard_map/ppermute | solution.py:246
  51.0 10.9 %collective-permute-done.6 = bf16[2,128,1024]{2,1,0:T(8,128)(2,1)S(1)} collective-permute-done((bf16[2,128,1024]{2,1,0:T(8,128)(2,1)S(1)}, bf16[2,128,1024]{2,1,0:T(8,128)(2,1)S(1)}, u32[]{:S(2)}, u32[]{:S(2)}) %collective-permute-start.6) | collective-permute-done | bytes 524320 | tf_op jit(solution)/shard_map/ppermute | solution.py:246
  61.9 0.0 collective-permute-done.7
  61.9 0.0 collective-permute-done.8
  61.9 0.4 add_convert_fusion
  62.4 0.8 %slice_bitcast_fusion = (bf16[128,1024]{1,0:T(8,128)(2,1)}, bf16[128,1024]{1,0:T(8,128)(2,1)}) fusion(bf16[2,128,1024]{2,1,0:T(8,128)(2,1)S(1)} %add_convert_fusion), kind=kLoop, calls=%fused_computation.2 | loop fusion | bytes 1048576 | tf_op jit(solution)/shard_map/squeeze | solution.py:288
  (13 shorter events, 0.0 us)
Async XLA Ops:
  0.6 22.8 %copy-start.8 = (f32[128,32]{0,1:T(8,128)S(1)}, f32[128,32]{0,1:T(8,128)}, u32[]{:S(2)}) copy-start(f32[128,32]{0,1:T(8,128)} %param.12) | copy-start | bytes 49156
  0.6 22.9 %copy-start.7 = (s32[4096]{0:T(1024)S(1)}, s32[4096]{0:T(1024)}, u32[]{:S(2)}) copy-start(s32[4096]{0:T(1024)} %param.13) | copy-start | bytes 49156
  0.7 22.9 %copy-start.1 = (bf16[128,4096]{1,0:T(8,128)(2,1)S(1)}, bf16[128,4096]{1,0:T(8,128)(2,1)}, u32[]{:S(2)}) copy-start(bf16[128,4096]{1,0:T(8,128)(2,1)} %refs_1_.3) | copy-start | bytes 3145732
  0.7 22.9 %copy-start = (bf16[128,4096]{1,0:T(8,128)(2,1)S(1)}, bf16[128,4096]{1,0:T(8,128)(2,1)}, u32[]{:S(2)}) copy-start(bf16[128,4096]{1,0:T(8,128)(2,1)} %refs_0_.3) | copy-start | bytes 3145732
  2.7 14.5 %collective-permute-start.1 = (bf16[2,128,1024]{2,1,0:T(8,128)(2,1)}, bf16[2,128,1024]{2,1,0:T(8,128)(2,1)S(1)}, u32[]{:S(2)}, u32[]{:S(2)}) collective-permute-start(bf16[2,128,1024]{2,1,0:T(8,128)(2,1)} %pad_maximum_fusion), channel_id=1, source_target_pairs={{0,16},{8,24},{16,1},{24,9},{1,17},{9,25},{17,2},{25,10},{2,18},{1... | collective-permute-start | bytes 1572872 | tf_op jit(solution)/shard_map/ppermute | solution.py:246
  5.7 13.1 %collective-permute-start = (bf16[2,128,1024]{2,1,0:T(8,128)(2,1)}, bf16[2,128,1024]{2,1,0:T(8,128)(2,1)S(1)}, u32[]{:S(2)}, u32[]{:S(2)}) collective-permute-start(bf16[2,128,1024]{2,1,0:T(8,128)(2,1)} %pad_maximum_fusion), channel_id=1, source_target_pairs={{0,8},{8,1},{16,24},{24,17},{1,9},{9,2},{17,25},{25,18},{2,10},{10... | collective-permute-start | bytes 1572872 | tf_op jit(solution)/shard_map/ppermute | solution.py:246
  7.2 22.8 %collective-permute-start.2 = (bf16[2,128,1024]{2,1,0:T(8,128)(2,1)}, bf16[2,128,1024]{2,1,0:T(8,128)(2,1)}, u32[]{:S(2)}, u32[]{:S(2)}) collective-permute-start(bf16[2,128,1024]{2,1,0:T(8,128)(2,1)} %pad_maximum_fusion), channel_id=1, source_target_pairs={{0,1},{8,9},{16,17},{24,25},{1,2},{9,10},{17,18},{25,26},{2,3},{10... | collective-permute-start | bytes 1572872 | tf_op jit(solution)/shard_map/ppermute | solution.py:246
  17.2 23.3 %collective-permute-start.3 = (bf16[1,128,1024]{2,1,0:T(8,128)(2,1)S(1)}, bf16[1,128,1024]{2,1,0:T(8,128)(2,1)S(1)}, u32[]{:S(2)}, u32[]{:S(2)}) collective-permute-start(bf16[1,128,1024]{2,1,0:T(8,128)(2,1)S(1)} %slice.16), channel_id=1, source_target_pairs={{16,24},{24,16},{1,9},{9,1},{17,25},{25,17},{2,10},{10,2},{18,26},... | collective-permute-start | bytes 786440 | tf_op jit(solution)/shard_map/ppermute | solution.py:246
  18.8 0.9 %copy-start.5 = (bf16[2,128,1024]{2,1,0:T(8,128)(2,1)}, bf16[2,128,1024]{2,1,0:T(8,128)(2,1)S(1)}, u32[]{:S(2)}) copy-start(bf16[2,128,1024]{2,1,0:T(8,128)(2,1)S(1)} %collective-permute-done.refs_6_) | copy-start | bytes 1572868
  19.7 20.8 %collective-permute-start.4 = (bf16[1,128,1024]{2,1,0:T(8,128)(2,1)}, bf16[1,128,1024]{2,1,0:T(8,128)(2,1)S(1)}, u32[]{:S(2)}, u32[]{:S(2)}) collective-permute-start(bf16[1,128,1024]{2,1,0:T(8,128)(2,1)} %slice.17), channel_id=1, source_target_pairs={{8,24},{1,16},{24,9},{17,1},{9,25},{2,17},{25,10},{18,2},{10,26},{... | collective-permute-start | bytes 786440 | tf_op jit(solution)/shard_map/ppermute | solution.py:246
  23.5 1.0 %copy-start.2 = (bf16[128,1024]{1,0:T(8,128)(2,1)S(1)}, bf16[128,1024]{1,0:T(8,128)(2,1)}, u32[]{:S(2)}) copy-start(bf16[128,1024]{1,0:T(8,128)(2,1)} %k_ref.1) | copy-start | bytes 786436
  24.5 0.9 %copy-start.3 = (bf16[128,1024]{1,0:T(8,128)(2,1)S(1)}, bf16[128,1024]{1,0:T(8,128)(2,1)}, u32[]{:S(2)}) copy-start(bf16[128,1024]{1,0:T(8,128)(2,1)} %v_ref.1) | copy-start | bytes 786436
  25.4 1.2 %copy-start.4 = (bf16[128,4096]{1,0:T(8,128)(2,1)S(1)}, bf16[128,4096]{1,0:T(8,128)(2,1)}, u32[]{:S(2)}) copy-start(bf16[128,4096]{1,0:T(8,128)(2,1)} %o_ref.1) | copy-start | bytes 3145732
  26.6 3.4 %copy-start.6 = (bf16[2,128,1024]{2,1,0:T(8,128)(2,1)S(1)}, bf16[2,128,1024]{2,1,0:T(8,128)(2,1)}, u32[]{:S(2)}) copy-start(bf16[2,128,1024]{2,1,0:T(8,128)(2,1)} %copy-done.5) | copy-start | bytes 1572868
  36.2 14.9 %collective-permute-start.5 = (bf16[2,128,1024]{2,1,0:T(8,128)(2,1)S(1)}, bf16[2,128,1024]{2,1,0:T(8,128)(2,1)S(1)}, u32[]{:S(2)}, u32[]{:S(2)}) collective-permute-start(bf16[2,128,1024]{2,1,0:T(8,128)(2,1)S(1)} %get-tuple-element.21), channel_id=1, source_target_pairs={{8,0},{1,8},{24,16},{17,24},{9,1},{2,9},{25,17},{18,25},{10,2},{3,... | collective-permute-start | bytes 1572872 | tf_op jit(solution)/shard_map/ppermute | solution.py:246
  37.0 24.9 %collective-permute-start.6 = (bf16[2,128,1024]{2,1,0:T(8,128)(2,1)S(1)}, bf16[2,128,1024]{2,1,0:T(8,128)(2,1)S(1)}, u32[]{:S(2)}, u32[]{:S(2)}) collective-permute-start(bf16[2,128,1024]{2,1,0:T(8,128)(2,1)S(1)} %get-tuple-element.22), channel_id=1, source_target_pairs={{16,0},{24,8},{1,16},{9,24},{17,1},{25,9},{2,17},{10,25},{18,2},{2... | collective-permute-start | bytes 1572872 | tf_op jit(solution)/shard_map/ppermute | solution.py:246
  38.6 23.3 %collective-permute-start.7 = (bf16[2,128,1024]{2,1,0:T(8,128)(2,1)S(1)}, bf16[2,128,1024]{2,1,0:T(8,128)(2,1)S(1)}, u32[]{:S(2)}, u32[]{:S(2)}) collective-permute-start(bf16[2,128,1024]{2,1,0:T(8,128)(2,1)S(1)} %get-tuple-element.23), channel_id=1, source_target_pairs={{1,0},{9,8},{17,16},{25,24},{2,1},{10,9},{18,17},{26,25},{3,2},{11... | collective-permute-start | bytes 1572872 | tf_op jit(solution)/shard_map/ppermute | solution.py:246
  44.4 17.5 %collective-permute-start.8 = (bf16[2,128,1024]{2,1,0:T(8,128)(2,1)S(1)}, bf16[2,128,1024]{2,1,0:T(8,128)(2,1)S(1)}, u32[]{:S(2)}, u32[]{:S(2)}) collective-permute-start(bf16[2,128,1024]{2,1,0:T(8,128)(2,1)S(1)} %get-tuple-element.24), channel_id=1, source_target_pairs={{24,0},{16,8},{9,16},{1,24},{25,1},{17,9},{10,17},{2,25},{26,2},{1... | collective-permute-start | bytes 1572872 | tf_op jit(solution)/shard_map/ppermute | solution.py:246
